TPU v7x, 32 devices: a whole 2x2x4 slice. The times are simulated.
32 devices in a mesh: parts: 2 (over y), row: 16 (over z, x, core).
Axes of the slice: x: 2, y: 2, z: 4, core: 2. Of those that a mesh axis runs over, the one named last changes fastest.
Arguments:
- traces: bfloat16 [256, 2, 12000], P(('parts', 'row')), parts along dimension 0, may hold values from -160 to 160
- valid_mask: int32 [256, 2], P(('parts', 'row')), parts along dimension 0, may hold values 0 or 1
- pair_table: int32 [32, 10], P(('parts', 'row')), parts along dimension 0, may hold values from 0 to 15, as said below
- stack_in: float32 [32, 10, 8, 8, 401], P(('parts', 'row')), parts along dimension 0, may hold values from -6 to 6
Outputs:
- stacks: float32 [32, 10, 8, 8, 401], P(('parts', 'row')), parts along dimension 0
There are 2 independent parts, one for each index of `parts`. A program takes and returns all parts, laid end to end along the dimension named above; each array names one. Nothing has to cross between parts.
Inputs may be any that keep to these rules, and one draw needn't show every extreme that they name: `pair_table`: row i lists the panels (i + k) mod 16 for k = -1 to 8, each once, in an order that varies from row to row.
All inputs are finite; a program needn't handle non-finite values. No bound on the sum of `valid_mask` on one device may be relied on, other than what follows from the above.
Results may differ from a plain program's by a relative error of at most 0.0032.
Values may be sent and summed in bfloat16 or wider, within the bound.
No kernel may reach another device: no remote copies, remote signals or barrier semaphores. Data moves between devices by JAX's collectives and lax.ppermute only.
A program may use at most 128 MiB of HBM per device.

v0:
```python
import math
import jax
import jax.numpy as jnp
from jax import lax
from jax.sharding import PartitionSpec as P

SAMPLES = 12000
FLO = 6
BINS = 595
HALF = 40
LAGS = 401
epsilon = 1e-06


def spectra_of(rows, samples, first_bin, bins):
    length = samples // 8
    freq = first_bin + jnp.arange(bins, dtype=jnp.int32)

    def absorb(totals, block_index):
        first_row = block_index * length
        segment = lax.dynamic_slice_in_dim(rows, first_row, length, 1)
        times = first_row + jnp.arange(length, dtype=jnp.int32)
        angle = (times[:, None] * freq[None, :] % samples).astype(jnp.float32) * (
            2.0 * math.pi / samples
        )
        table = jnp.concatenate([jnp.cos(angle), -jnp.sin(angle)], axis=1).astype(jnp.bfloat16)
        return (totals + jnp.dot(segment, table, preferred_element_type=jnp.float32), None)

    start_total = jnp.zeros((rows.shape[0], 2 * bins), jnp.float32)
    totals, unused = lax.scan(absorb, start_total, jnp.arange(8, dtype=jnp.int32))
    return totals


def whiten_rows(traces, valid_mask, first_bin, bins, half_width):
    chans, minutes, samples = traces.shape
    spectrum = spectra_of(traces.reshape(chans * minutes, samples), samples, first_bin, bins)
    real_part = spectrum[:, :bins]
    imag_part = spectrum[:, bins:]
    power = real_part * real_part + imag_part * imag_part
    positions = jnp.arange(bins, dtype=jnp.int32)
    near = (jnp.abs(positions[:, None] - positions[None, :]) <= half_width).astype(jnp.float32)
    window = near / jnp.sum(near, axis=0, keepdims=True)
    smooth = jnp.dot(power, window, precision=lax.Precision.HIGHEST)
    divisor = jnp.sqrt(smooth + epsilon)
    flags = valid_mask.reshape(-1, 1).astype(jnp.float32)
    whitened = spectrum * flags / jnp.concatenate([divisor, divisor], axis=1)
    return whitened.astype(jnp.bfloat16).reshape(chans, minutes, 2 * bins)


def lag_matrix(first_bin, bins, lags, samples):
    freq = first_bin + jnp.arange(bins, dtype=jnp.int32)
    shifts = jnp.arange(lags, dtype=jnp.int32) - (lags - 1) // 2
    angle = (freq[:, None] * shifts[None, :] % samples).astype(jnp.float32) * (
        2.0 * math.pi / samples
    )
    return jnp.concatenate([jnp.cos(angle), -jnp.sin(angle)], axis=0).astype(jnp.bfloat16)


def tile_corr(own_white, own_flags, partner_white, partner_flags, lag_table):
    bins = lag_table.shape[0] // 2
    own = own_white.astype(jnp.float32)
    partner = partner_white.astype(jnp.float32)
    shape = (partner.shape[0], own.shape[0], partner.shape[1], bins)
    real_sum = jnp.zeros(shape, jnp.float32)
    imag_sum = jnp.zeros(shape, jnp.float32)
    joint_sum = jnp.zeros(shape[:3], jnp.float32)
    for minute in range(own.shape[1]):
        own_real = own[:, minute, :bins][None, :, None, :]
        own_imag = own[:, minute, bins:][None, :, None, :]
        part_real = partner[:, :, minute, :bins][:, None, :, :]
        part_imag = partner[:, :, minute, bins:][:, None, :, :]
        real_sum = real_sum + (own_real * part_real + own_imag * part_imag)
        imag_sum = imag_sum + (own_imag * part_real - own_real * part_imag)
        own_valid = own_flags[:, minute].astype(jnp.float32)[None, :, None]
        part_valid = partner_flags[:, :, minute].astype(jnp.float32)[:, None, :]
        joint_sum = joint_sum + own_valid * part_valid
    inverse = 1.0 / jnp.maximum(joint_sum, 1.0)
    cross = (jnp.concatenate([real_sum, imag_sum], axis=-1) * inverse[..., None]).astype(
        jnp.bfloat16
    )
    corr = jnp.dot(cross.reshape(-1, 2 * bins), lag_table, preferred_element_type=jnp.float32) * (
        1.0 / math.sqrt(bins)
    )
    return corr.reshape(shape[0], shape[1], shape[2], lag_table.shape[1])


def shards(traces, valid_mask, pair_table, stack_in):
    panel_count = lax.axis_size("row")
    chans = traces.shape[0]
    minutes = traces.shape[1]
    whitened = whiten_rows(traces, valid_mask, FLO, BINS, HALF)
    own_flags = valid_mask.astype(jnp.bfloat16)
    lag_table = lag_matrix(FLO, BINS, LAGS, SAMPLES)
    table_row = pair_table[0]
    base_stack = stack_in[0]
    whole_white, whole_flags = (
        lax.all_gather(whitened, "row", axis=0, tiled=True),
        lax.all_gather(own_flags, "row", axis=0, tiled=True),
    )
    panels = whole_white.reshape(panel_count, chans, minutes, whitened.shape[2])
    panel_flags = whole_flags.reshape(panel_count, chans, minutes)
    partner = jnp.take(panels, table_row, axis=0)
    partner_flags = jnp.take(panel_flags, table_row, axis=0)
    result = base_stack + tile_corr(whitened, own_flags, partner, partner_flags, lag_table)
    return result[None]


def solution(mesh):
    in_specs = (
        P(("parts", "row"), None, None),
        P(("parts", "row"), None),
        P(("parts", "row"), None),
        P(("parts", "row"), None, None, None, None),
    )
    out_specs = P(("parts", "row"), None, None, None, None)
    return jax.shard_map(shards, mesh=mesh, in_specs=in_specs, out_specs=out_specs, check_vma=False)
```

profile of v0, /device:TPU:0, one launch (start us, length us, event | category | flops | bytes accessed | tf_op | source)
XLA Modules:
  0.0 214.5 jit_solution(12585721607296174629)
XLA Ops:
  0.0 0.7 compare_and_fusion
  0.7 0.7 fusion.46
  1.3 0.8 fusion.52
  2.4 23.0 %all-gather = bf16[16,8,2]{1,2,0:T(2,128)(2,1)S(1)} all-gather(bf16[1,8,2]{1,2,0:T(2,128)(2,1)S(1)} %bitcast.50), channel_id=1, replica_groups=mesh['parts'=2,'row'=16] {'row'}, dimensions={0}, use_global_device_ids=true | all-gather | bytes 544 | tf_op jit(solution)/shard_map/all_gather | solution.py:98
  26.4 1.3 reshape.162
  27.7 151.3 %while.13 = (s32[]{:T(128)}, f32[16,1190]{1,0:T(8,128)S(1)}, s32[8]{0:T(128)S(1)}, bf16[16,12000]{1,0:T(8,128)(2,1)S(1)}, s32[]{:T(128)}, /*index=5*/s32[1]{0:T(128)}, s32[]{:T(128)}, s32[]{:T(128)}) while((s32[]{:T(128)}, f32[16,1190]{1,0:T(8,128)S(1)}, s32[8]{0:T(128)S(1)}, bf16[16,12000]{1,0:T(8,128)(2,1)S(1)}, s32[]{:T(128)}, ...), condition=%wide.region_1.2_spmd.clone, body=%wide.region_0.1_spmd.clone.sunk | while | flops 75010184 | bytes 7644401 | solution.py:30
  27.7 0.7 dynamic_slice.20
  29.0 16.6 %cosine_convert_fusion.3 = (bf16[1500,595]{1,0:T(8,128)(2,1)S(1)}, bf16[1500,595]{1,0:T(8,128)(2,1)S(1)}) fusion(s32[595]{0:T(1024)S(1)} %iota_add_fusion.6, s32[1500]{0:T(1024)S(1)} %iota_add_fusion.7), kind=kLoop, calls=%fused_computation.11.clone.1 | loop fusion | flops 10710000 | bytes 3578380 | tf_op jit(solution)/shard_map/convert
  45.6 1.0 fusion.58
  47.9 16.6 %cosine_convert_fusion.3 = (bf16[1500,595]{1,0:T(8,128)(2,1)S(1)}, bf16[1500,595]{1,0:T(8,128)(2,1)S(1)}) fusion(s32[595]{0:T(1024)S(1)} %iota_add_fusion.6, s32[1500]{0:T(1024)S(1)} %iota_add_fusion.7), kind=kLoop, calls=%fused_computation.11.clone.1 | loop fusion | flops 10710000 | bytes 3578380 | tf_op jit(solution)/shard_map/convert
  64.5 1.0 fusion.58
  66.8 16.6 %cosine_convert_fusion.3 = (bf16[1500,595]{1,0:T(8,128)(2,1)S(1)}, bf16[1500,595]{1,0:T(8,128)(2,1)S(1)}) fusion(s32[595]{0:T(1024)S(1)} %iota_add_fusion.6, s32[1500]{0:T(1024)S(1)} %iota_add_fusion.7), kind=kLoop, calls=%fused_computation.11.clone.1 | loop fusion | flops 10710000 | bytes 3578380 | tf_op jit(solution)/shard_map/convert
  83.4 1.0 fusion.58
  85.7 16.6 %cosine_convert_fusion.3 = (bf16[1500,595]{1,0:T(8,128)(2,1)S(1)}, bf16[1500,595]{1,0:T(8,128)(2,1)S(1)}) fusion(s32[595]{0:T(1024)S(1)} %iota_add_fusion.6, s32[1500]{0:T(1024)S(1)} %iota_add_fusion.7), kind=kLoop, calls=%fused_computation.11.clone.1 | loop fusion | flops 10710000 | bytes 3578380 | tf_op jit(solution)/shard_map/convert
  102.3 1.0 fusion.58
  104.6 16.6 %cosine_convert_fusion.3 = (bf16[1500,595]{1,0:T(8,128)(2,1)S(1)}, bf16[1500,595]{1,0:T(8,128)(2,1)S(1)}) fusion(s32[595]{0:T(1024)S(1)} %iota_add_fusion.6, s32[1500]{0:T(1024)S(1)} %iota_add_fusion.7), kind=kLoop, calls=%fused_computation.11.clone.1 | loop fusion | flops 10710000 | bytes 3578380 | tf_op jit(solution)/shard_map/convert
  121.2 1.0 fusion.58
  123.5 16.6 %cosine_convert_fusion.3 = (bf16[1500,595]{1,0:T(8,128)(2,1)S(1)}, bf16[1500,595]{1,0:T(8,128)(2,1)S(1)}) fusion(s32[595]{0:T(1024)S(1)} %iota_add_fusion.6, s32[1500]{0:T(1024)S(1)} %iota_add_fusion.7), kind=kLoop, calls=%fused_computation.11.clone.1 | loop fusion | flops 10710000 | bytes 3578380 | tf_op jit(solution)/shard_map/convert
  140.1 1.0 fusion.58
  142.4 16.6 %cosine_convert_fusion.3 = (bf16[1500,595]{1,0:T(8,128)(2,1)S(1)}, bf16[1500,595]{1,0:T(8,128)(2,1)S(1)}) fusion(s32[595]{0:T(1024)S(1)} %iota_add_fusion.6, s32[1500]{0:T(1024)S(1)} %iota_add_fusion.7), kind=kLoop, calls=%fused_computation.11.clone.1 | loop fusion | flops 10710000 | bytes 3578380 | tf_op jit(solution)/shard_map/convert
  159.0 1.0 fusion.58
  161.4 16.6 %cosine_convert_fusion.3 = (bf16[1500,595]{1,0:T(8,128)(2,1)S(1)}, bf16[1500,595]{1,0:T(8,128)(2,1)S(1)}) fusion(s32[595]{0:T(1024)S(1)} %iota_add_fusion.6, s32[1500]{0:T(1024)S(1)} %iota_add_fusion.7), kind=kLoop, calls=%fused_computation.11.clone.1 | loop fusion | flops 10710000 | bytes 3578380 | tf_op jit(solution)/shard_map/convert
  177.9 1.0 fusion.58
  179.0 0.8 fusion.34
  180.1 19.4 %all_gather.6 = bf16[128,2,1190]{2,1,0:T(2,128)(2,1)S(1)} all-gather(bf16[8,2,1190]{2,1,0:T(2,128)(2,1)S(1)} %reshape.163), channel_id=1, replica_groups=mesh['parts'=2,'row'=16] {'row'}, dimensions={0}, use_global_device_ids=true | all-gather | bytes 647360 | tf_op jit(solution)/shard_map/all_gather | solution.py:97
  199.4 1.4 gather_fusion
  201.3 1.2 fusion.50
  202.6 5.6 %cosine_convert_fusion.1 = (bf16[595,401]{1,0:T(8,128)(2,1)S(1)}, bf16[595,401]{1,0:T(8,128)(2,1)S(1)}) fusion(s32[401]{0:T(512)S(1)} %iota_add_fusion.3, s32[595]{0:T(1024)S(1)} %iota_add_fusion.2), kind=kLoop, calls=%fused_computation.37 | loop fusion | flops 2863140 | bytes 958364 | tf_op jit(solution)/shard_map/convert.6
  208.1 0.8 add_add_fusion
  208.9 2.4 %fusion.22 = f32[640,401]{0,1:T(8,128)} fusion(f32[640,595]{1,0:T(8,128)S(1)} %bitcast.49, f32[640,595]{1,0:T(8,128)S(1)} %bitcast.48, f32[640]{0:T(1024)S(1)} %div.25, bf16[595,401]{1,0:T(8,128)(2,1)S(1)} %get-tuple-element.110, bf16[595,401]{1,0:T(8,128)(2,1)S(1)} %get-tuple-element.109), kind=kOutput, calls=%fused_computation.33 | convolution fusion | flops 615253376 | bytes 5029900 | tf_op jit(solution)/shard_map/dot_general | solution.py:81
  211.3 1.7 copy.37
  213.1 1.4 add.141
  (50 shorter events, 6.7 us)
Async XLA Ops:
  211.3 1.7 copy-start
where the time goes:
time: 215 us; the launch traced here: 214 us
  other arithmetic  143 us (67%)
  blocking collectives  42.3 us (20%)
  local copies, waits for them, and re-layouts  12.1 us (6%)
  matrix products  11.3 us (5%)
  loops' own time  5.26 us (2%)
    another operation x9, other arithmetic  138 us
    all_gather x1, blocking collectives, shards(): lax.all_gather(own_flags, 'row', axis=0, tiled=True)  23 us
    all_gather x1, blocking collectives, shards(): lax.all_gather(whitened, 'row', axis=0, tiled=True)  19.4 us
    dot_general x8, matrix products, absorb(): jnp.dot(segment, table, preferred_element_type=jnp.float32)  8.12 us
    another operation x1, loops' own time, spectra_of(): lax.scan(absorb, start_total, jnp.arange(8, dtype=jnp.int32))  5.26 us
    dynamic_slice x8, local copies, waits for them, and re-layouts, spectra_of(): lax.scan(absorb, start_total, jnp.arange(8, dtype=jnp.int32))  5.19 us

commit v1 on v0

--- a/solution.py
+++ b/solution.py
@@ -10,6 +10,20 @@
 HALF = 40
 LAGS = 401
 epsilon = 1e-06
+
+
+def direct_core_by_axis(u_in):
+    axis_name = "row"
+    slots = lax.axis_size(axis_name)
+    heap = list(map(lambda u: (u, (u + 1) % slots), range(slots)))
+    pieces_in = list(map(lambda u: (u, (u - 1) % slots), range(slots)))
+    fresh, arr_out = ([u_in], [u_in])
+    for _ in range(slots // 2):
+        fresh.append(lax.ppermute(fresh[-1], axis_name, heap))
+    for _ in [*range((slots - 1) // 2)]:
+        arr_out.append(lax.ppermute(arr_out[-1], axis_name, pieces_in))
+    top = jnp.concatenate([*fresh[::-1], *arr_out[1:]], axis=0)
+    return jnp.roll(top, (lax.axis_index(axis_name) - slots // 2) * u_in.shape[0], axis=0)
 
 
 def spectra_of(rows, samples, first_bin, bins):
@@ -95,7 +109,7 @@
     base_stack = stack_in[0]
     whole_white, whole_flags = (
         lax.all_gather(whitened, "row", axis=0, tiled=True),
-        lax.all_gather(own_flags, "row", axis=0, tiled=True),
+        direct_core_by_axis(own_flags),
     )
     panels = whole_white.reshape(panel_count, chans, minutes, whitened.shape[2])
     panel_flags = whole_flags.reshape(panel_count, chans, minutes)

time: 215 us -> 240 us (1.12)
  starting transfers between devices: 0 us -> 28 us
  blocking collectives: 42.3 us -> 20.5 us
  waiting for transfers between devices: 0 us -> 17.8 us
    ppermute x0 -> x15, starting transfers between devices: none -> 28 us  [the longest x7 28 us: direct_core_by_axis(): arr_out.append(lax.ppermute(arr_out[-1], axis_name, pieces_in))]
    all_gather x1 -> x0, blocking collectives: 23 us -> none  [shards(): lax.all_gather(own_flags, 'row', axis=0, tiled=True)]
    ppermute x0 -> x15, waiting for transfers between devices: none -> 17.8 us  [the longest x8 11.3 us: direct_core_by_axis(): fresh.append(lax.ppermute(fresh[-1], axis_name, heap))]
  transfers between devices with their start and end apart: 0 -> 15, of which waited for: 0 -> 7; matrix products, arithmetic and copies ran while one was open for 0% -> 67% of each run, Pallas kernels for 0% -> 0%
where the time goes in v1:
time: 240 us
  other arithmetic  144 us (60%)
  starting transfers between devices  28 us (12%)
  blocking collectives  20.5 us (9%)
  waiting for transfers between devices  17.8 us (7%)
  matrix products  12.5 us (5%)
  local copies, waits for them, and re-layouts  11.9 us (5%)
  loops' own time  4.85 us (2%)
    another operation x9, other arithmetic  139 us
    ppermute x7, starting transfers between devices, direct_core_by_axis(): arr_out.append(lax.ppermute(arr_out[-1], axis_name, pieces_in))  28 us
    all_gather x1, blocking collectives, shards(): lax.all_gather(whitened, 'row', axis=0, tiled=True)  20.5 us
    ppermute x8, waiting for transfers between devices, direct_core_by_axis(): fresh.append(lax.ppermute(fresh[-1], axis_name, heap))  11.3 us
    dot_general x8, matrix products, absorb(): jnp.dot(segment, table, preferred_element_type=jnp.float32)  8.12 us
    ppermute x7, waiting for transfers between devices, direct_core_by_axis(): arr_out.append(lax.ppermute(arr_out[-1], axis_name, pieces_in))  6.45 us
    another operation x1, loops' own time, spectra_of(): lax.scan(absorb, start_total, jnp.arange(8, dtype=jnp.int32))  4.85 us
  transfers between devices with their start and end apart: 15, of which 7 were waited for; matrix products, arithmetic and copies ran while one was open for 67% of the time, Pallas kernels for 0%

profile of v1, /device:TPU:0, one launch (start us, length us, event | category | flops | bytes accessed | tf_op | source)
XLA Modules:
  0.0 239.8 jit_solution(4885862779120431734)
XLA Ops:
  0.8 5.4 %collective-permute-start.8 = (bf16[8,2]{0,1:T(2,128)(2,1)S(1)}, bf16[8,2]{0,1:T(2,128)(2,1)S(1)}, u32[]{:S(2)}, u32[]{:S(2)}) collective-permute-start(bf16[8,2]{0,1:T(2,128)(2,1)S(1)} %get-tuple-element.113), channel_id=1, source_target_pairs={{0,15},{1,0},{2,1},{3,2},{4,3},{5,4},{6,5},{7,6},{8,7},{9,8},{10,9... | collective-permute-start | bytes 104 | tf_op jit(solution)/shard_map/ppermute | solution.py:24
  7.8 1.3 reshape.162
  9.1 150.4 %while.13 = (s32[]{:T(128)}, f32[16,1190]{1,0:T(8,128)S(1)}, s32[8]{0:T(128)S(1)}, bf16[16,12000]{1,0:T(8,128)(2,1)S(1)}, s32[]{:T(128)}, /*index=5*/s32[1]{0:T(128)}, s32[]{:T(128)}, s32[]{:T(128)}) while((s32[]{:T(128)}, f32[16,1190]{1,0:T(8,128)S(1)}, s32[8]{0:T(128)S(1)}, bf16[16,12000]{1,0:T(8,128)(2,1)S(1)}, s32[]{:T(128)}, ...), condition=%wide.region_1.2_spmd.clone, body=%wide.region_0.1_spmd.clone.sunk | while | flops 75010184 | bytes 7644401 | solution.py:44
  10.3 16.6 %cosine_convert_fusion.3 = (bf16[1500,595]{1,0:T(8,128)(2,1)S(1)}, bf16[1500,595]{1,0:T(8,128)(2,1)S(1)}) fusion(s32[595]{0:T(1024)S(1)} %iota_add_fusion.6, s32[1500]{0:T(1024)S(1)} %iota_add_fusion.7), kind=kLoop, calls=%fused_computation.11.clone.1 | loop fusion | flops 10710000 | bytes 3578380 | tf_op jit(solution)/shard_map/convert
  29.1 16.6 %cosine_convert_fusion.3 = (bf16[1500,595]{1,0:T(8,128)(2,1)S(1)}, bf16[1500,595]{1,0:T(8,128)(2,1)S(1)}) fusion(s32[595]{0:T(1024)S(1)} %iota_add_fusion.6, s32[1500]{0:T(1024)S(1)} %iota_add_fusion.7), kind=kLoop, calls=%fused_computation.11.clone.1 | loop fusion | flops 10710000 | bytes 3578380 | tf_op jit(solution)/shard_map/convert
  47.9 16.6 %cosine_convert_fusion.3 = (bf16[1500,595]{1,0:T(8,128)(2,1)S(1)}, bf16[1500,595]{1,0:T(8,128)(2,1)S(1)}) fusion(s32[595]{0:T(1024)S(1)} %iota_add_fusion.6, s32[1500]{0:T(1024)S(1)} %iota_add_fusion.7), kind=kLoop, calls=%fused_computation.11.clone.1 | loop fusion | flops 10710000 | bytes 3578380 | tf_op jit(solution)/shard_map/convert
  64.5 1.0 fusion.58
  66.7 16.6 %cosine_convert_fusion.3 = (bf16[1500,595]{1,0:T(8,128)(2,1)S(1)}, bf16[1500,595]{1,0:T(8,128)(2,1)S(1)}) fusion(s32[595]{0:T(1024)S(1)} %iota_add_fusion.6, s32[1500]{0:T(1024)S(1)} %iota_add_fusion.7), kind=kLoop, calls=%fused_computation.11.clone.1 | loop fusion | flops 10710000 | bytes 3578380 | tf_op jit(solution)/shard_map/convert
  85.5 16.6 %cosine_convert_fusion.3 = (bf16[1500,595]{1,0:T(8,128)(2,1)S(1)}, bf16[1500,595]{1,0:T(8,128)(2,1)S(1)}) fusion(s32[595]{0:T(1024)S(1)} %iota_add_fusion.6, s32[1500]{0:T(1024)S(1)} %iota_add_fusion.7), kind=kLoop, calls=%fused_computation.11.clone.1 | loop fusion | flops 10710000 | bytes 3578380 | tf_op jit(solution)/shard_map/convert
  102.1 1.0 fusion.58
  104.3 16.6 %cosine_convert_fusion.3 = (bf16[1500,595]{1,0:T(8,128)(2,1)S(1)}, bf16[1500,595]{1,0:T(8,128)(2,1)S(1)}) fusion(s32[595]{0:T(1024)S(1)} %iota_add_fusion.6, s32[1500]{0:T(1024)S(1)} %iota_add_fusion.7), kind=kLoop, calls=%fused_computation.11.clone.1 | loop fusion | flops 10710000 | bytes 3578380 | tf_op jit(solution)/shard_map/convert
  123.1 16.6 %cosine_convert_fusion.3 = (bf16[1500,595]{1,0:T(8,128)(2,1)S(1)}, bf16[1500,595]{1,0:T(8,128)(2,1)S(1)}) fusion(s32[595]{0:T(1024)S(1)} %iota_add_fusion.6, s32[1500]{0:T(1024)S(1)} %iota_add_fusion.7), kind=kLoop, calls=%fused_computation.11.clone.1 | loop fusion | flops 10710000 | bytes 3578380 | tf_op jit(solution)/shard_map/convert
  141.9 16.6 %cosine_convert_fusion.3 = (bf16[1500,595]{1,0:T(8,128)(2,1)S(1)}, bf16[1500,595]{1,0:T(8,128)(2,1)S(1)}) fusion(s32[595]{0:T(1024)S(1)} %iota_add_fusion.6, s32[1500]{0:T(1024)S(1)} %iota_add_fusion.7), kind=kLoop, calls=%fused_computation.11.clone.1 | loop fusion | flops 10710000 | bytes 3578380 | tf_op jit(solution)/shard_map/convert
  160.6 20.5 %all_gather.3 = bf16[128,2,1190]{2,1,0:T(2,128)(2,1)S(1)} all-gather(bf16[8,2,1190]{2,1,0:T(2,128)(2,1)S(1)} %reshape.163), channel_id=1, replica_groups=mesh['parts'=2,'row'=16] {'row'}, dimensions={0}, use_global_device_ids=true | all-gather | bytes 647360 | tf_op jit(solution)/shard_map/all_gather | solution.py:111
  181.0 1.4 gather_fusion
  182.9 1.2 fusion.50
  184.2 6.3 %cosine_convert_fusion.1 = (bf16[595,401]{1,0:T(8,128)(2,1)}, bf16[595,401]{1,0:T(8,128)(2,1)}) fusion(s32[401]{0:T(512)S(1)} %iota_add_fusion.3, s32[595]{0:T(1024)S(1)} %iota_add_fusion.2), kind=kLoop, calls=%fused_computation.37 | loop fusion | flops 2863140 | bytes 958364 | tf_op jit(solution)/shard_map/convert.6
  192.0 1.3 collective-permute-done.9
  193.3 4.4 %collective-permute-start.10 = (bf16[8,2]{0,1:T(2,128)(2,1)S(1)}, bf16[8,2]{0,1:T(2,128)(2,1)S(1)}, u32[]{:S(2)}, u32[]{:S(2)}) collective-permute-start(bf16[8,2]{0,1:T(2,128)(2,1)S(1)} %collective-permute-done.9), channel_id=1, source_target_pairs={{0,15},{1,0},{2,1},{3,2},{4,3},{5,4},{6,5},{7,6},{8,7},{9,8},{10,9... | collective-permute-start | bytes 104 | tf_op jit(solution)/shard_map/ppermute | solution.py:24
  197.7 1.3 collective-permute-done.10
  199.0 4.4 %collective-permute-start.11 = (bf16[8,2]{0,1:T(2,128)(2,1)S(1)}, bf16[8,2]{0,1:T(2,128)(2,1)S(1)}, u32[]{:S(2)}, u32[]{:S(2)}) collective-permute-start(bf16[8,2]{0,1:T(2,128)(2,1)S(1)} %collective-permute-done.10), channel_id=1, source_target_pairs={{0,15},{1,0},{2,1},{3,2},{4,3},{5,4},{6,5},{7,6},{8,7},{9,8},{10,9... | collective-permute-start | bytes 104 | tf_op jit(solution)/shard_map/ppermute | solution.py:24
  203.3 1.3 collective-permute-done.11
  204.6 4.4 %collective-permute-start.12 = (bf16[8,2]{0,1:T(2,128)(2,1)S(1)}, bf16[8,2]{0,1:T(2,128)(2,1)S(1)}, u32[]{:S(2)}, u32[]{:S(2)}) collective-permute-start(bf16[8,2]{0,1:T(2,128)(2,1)S(1)} %collective-permute-done.11), channel_id=1, source_target_pairs={{0,15},{1,0},{2,1},{3,2},{4,3},{5,4},{6,5},{7,6},{8,7},{9,8},{10,9... | collective-permute-start | bytes 104 | tf_op jit(solution)/shard_map/ppermute | solution.py:24
  209.0 1.3 collective-permute-done.12
  210.3 4.4 %collective-permute-start.13 = (bf16[8,2]{0,1:T(2,128)(2,1)S(1)}, bf16[8,2]{0,1:T(2,128)(2,1)S(1)}, u32[]{:S(2)}, u32[]{:S(2)}) collective-permute-start(bf16[8,2]{0,1:T(2,128)(2,1)S(1)} %collective-permute-done.12), channel_id=1, source_target_pairs={{0,15},{1,0},{2,1},{3,2},{4,3},{5,4},{6,5},{7,6},{8,7},{9,8},{10,9... | collective-permute-start | bytes 104 | tf_op jit(solution)/shard_map/ppermute | solution.py:24
  214.7 1.3 collective-permute-done.13
  216.0 4.4 %collective-permute-start.14 = (bf16[8,2]{0,1:T(2,128)(2,1)S(1)}, bf16[8,2]{0,1:T(2,128)(2,1)S(1)}, u32[]{:S(2)}, u32[]{:S(2)}) collective-permute-start(bf16[8,2]{0,1:T(2,128)(2,1)S(1)} %collective-permute-done.13), channel_id=1, source_target_pairs={{0,15},{1,0},{2,1},{3,2},{4,3},{5,4},{6,5},{7,6},{8,7},{9,8},{10,9... | collective-permute-start | bytes 104 | tf_op jit(solution)/shard_map/ppermute | solution.py:24
  220.3 5.7 %collective-permute-done.6 = bf16[8,2]{0,1:T(2,128)(2,1)S(1)} collective-permute-done((bf16[8,2]{0,1:T(2,128)(2,1)S(1)}, bf16[8,2]{0,1:T(2,128)(2,1)S(1)}, u32[]{:S(2)}, u32[]{:S(2)}) %collective-permute-start.6) | collective-permute-done | bytes 64 | tf_op jit(solution)/shard_map/ppermute | solution.py:22
  226.0 5.7 %collective-permute-done.7 = bf16[8,2]{0,1:T(2,128)(2,1)S(1)} collective-permute-done((bf16[8,2]{0,1:T(2,128)(2,1)S(1)}, bf16[8,2]{0,1:T(2,128)(2,1)S(1)}, u32[]{:S(2)}, u32[]{:S(2)}) %collective-permute-start.7) | collective-permute-done | bytes 64 | tf_op jit(solution)/shard_map/ppermute | solution.py:22
  233.0 3.6 %fusion.22 = f32[640,401]{0,1:T(8,128)} fusion(f32[640,595]{1,0:T(8,128)S(1)} %bitcast.50, f32[640,595]{1,0:T(8,128)S(1)} %bitcast.49, f32[640]{0:T(1024)S(1)} %div.25, bf16[595,401]{1,0:T(8,128)(2,1)} %get-tuple-element.110, bf16[595,401]{1,0:T(8,128)(2,1)} %get-tuple-element.109), kind=kOutput, calls=%fused_computation.33 | convolution fusion | flops 615253376 | bytes 5029900 | tf_op jit(solution)/shard_map/dot_general | solution.py:95
  236.6 1.7 copy.35
  238.3 1.4 add.154
  (83 shorter events, 17.7 us)
Async XLA Ops:
  0.8 190.5 %collective-permute-start.8 = (bf16[8,2]{0,1:T(2,128)(2,1)S(1)}, bf16[8,2]{0,1:T(2,128)(2,1)S(1)}, u32[]{:S(2)}, u32[]{:S(2)}) collective-permute-start(bf16[8,2]{0,1:T(2,128)(2,1)S(1)} %get-tuple-element.113), channel_id=1, source_target_pairs={{0,15},{1,0},{2,1},{3,2},{4,3},{5,4},{6,5},{7,6},{8,7},{9,8},{10,9... | collective-permute-start | bytes 104 | tf_op jit(solution)/shard_map/ppermute | solution.py:24
  6.2 185.8 %collective-permute-start = (bf16[8,2]{0,1:T(2,128)(2,1)S(1)}, bf16[8,2]{0,1:T(2,128)(2,1)S(1)}, u32[]{:S(2)}, u32[]{:S(2)}) collective-permute-start(bf16[8,2]{0,1:T(2,128)(2,1)S(1)} %get-tuple-element.113), channel_id=1, source_target_pairs={{0,1},{1,2},{2,3},{3,4},{4,5},{5,6},{6,7},{7,8},{8,9},{9,10},{10,1... | collective-permute-start | bytes 104 | tf_op jit(solution)/shard_map/ppermute | solution.py:22
  191.2 2.1 collective-permute-start.9
  192.0 5.7 %collective-permute-start.1 = (bf16[8,2]{0,1:T(2,128)(2,1)S(1)}, bf16[8,2]{0,1:T(2,128)(2,1)S(1)}, u32[]{:S(2)}, u32[]{:S(2)}) collective-permute-start(bf16[8,2]{0,1:T(2,128)(2,1)S(1)} %collective-permute-done), channel_id=1, source_target_pairs={{0,1},{1,2},{2,3},{3,4},{4,5},{5,6},{6,7},{7,8},{8,9},{9,10},{10,1... | collective-permute-start | bytes 104 | tf_op jit(solution)/shard_map/ppermute | solution.py:22
  193.3 5.7 %collective-permute-start.10 = (bf16[8,2]{0,1:T(2,128)(2,1)S(1)}, bf16[8,2]{0,1:T(2,128)(2,1)S(1)}, u32[]{:S(2)}, u32[]{:S(2)}) collective-permute-start(bf16[8,2]{0,1:T(2,128)(2,1)S(1)} %collective-permute-done.9), channel_id=1, source_target_pairs={{0,15},{1,0},{2,1},{3,2},{4,3},{5,4},{6,5},{7,6},{8,7},{9,8},{10,9... | collective-permute-start | bytes 104 | tf_op jit(solution)/shard_map/ppermute | solution.py:24
  197.7 5.7 %collective-permute-start.2 = (bf16[8,2]{0,1:T(2,128)(2,1)S(1)}, bf16[8,2]{0,1:T(2,128)(2,1)S(1)}, u32[]{:S(2)}, u32[]{:S(2)}) collective-permute-start(bf16[8,2]{0,1:T(2,128)(2,1)S(1)} %collective-permute-done.1), channel_id=1, source_target_pairs={{0,1},{1,2},{2,3},{3,4},{4,5},{5,6},{6,7},{7,8},{8,9},{9,10},{10,1... | collective-permute-start | bytes 104 | tf_op jit(solution)/shard_map/ppermute | solution.py:22
  199.0 5.7 %collective-permute-start.11 = (bf16[8,2]{0,1:T(2,128)(2,1)S(1)}, bf16[8,2]{0,1:T(2,128)(2,1)S(1)}, u32[]{:S(2)}, u32[]{:S(2)}) collective-permute-start(bf16[8,2]{0,1:T(2,128)(2,1)S(1)} %collective-permute-done.10), channel_id=1, source_target_pairs={{0,15},{1,0},{2,1},{3,2},{4,3},{5,4},{6,5},{7,6},{8,7},{9,8},{10,9... | collective-permute-start | bytes 104 | tf_op jit(solution)/shard_map/ppermute | solution.py:24
  203.3 5.7 %collective-permute-start.3 = (bf16[8,2]{0,1:T(2,128)(2,1)S(1)}, bf16[8,2]{0,1:T(2,128)(2,1)S(1)}, u32[]{:S(2)}, u32[]{:S(2)}) collective-permute-start(bf16[8,2]{0,1:T(2,128)(2,1)S(1)} %collective-permute-done.2), channel_id=1, source_target_pairs={{0,1},{1,2},{2,3},{3,4},{4,5},{5,6},{6,7},{7,8},{8,9},{9,10},{10,1... | collective-permute-start | bytes 104 | tf_op jit(solution)/shard_map/ppermute | solution.py:22
  204.6 5.7 %collective-permute-start.12 = (bf16[8,2]{0,1:T(2,128)(2,1)S(1)}, bf16[8,2]{0,1:T(2,128)(2,1)S(1)}, u32[]{:S(2)}, u32[]{:S(2)}) collective-permute-start(bf16[8,2]{0,1:T(2,128)(2,1)S(1)} %collective-permute-done.11), channel_id=1, source_target_pairs={{0,15},{1,0},{2,1},{3,2},{4,3},{5,4},{6,5},{7,6},{8,7},{9,8},{10,9... | collective-permute-start | bytes 104 | tf_op jit(solution)/shard_map/ppermute | solution.py:24
  209.0 5.7 %collective-permute-start.4 = (bf16[8,2]{0,1:T(2,128)(2,1)S(1)}, bf16[8,2]{0,1:T(2,128)(2,1)S(1)}, u32[]{:S(2)}, u32[]{:S(2)}) collective-permute-start(bf16[8,2]{0,1:T(2,128)(2,1)S(1)} %collective-permute-done.3), channel_id=1, source_target_pairs={{0,1},{1,2},{2,3},{3,4},{4,5},{5,6},{6,7},{7,8},{8,9},{9,10},{10,1... | collective-permute-start | bytes 104 | tf_op jit(solution)/shard_map/ppermute | solution.py:22
  210.3 5.7 %collective-permute-start.13 = (bf16[8,2]{0,1:T(2,128)(2,1)S(1)}, bf16[8,2]{0,1:T(2,128)(2,1)S(1)}, u32[]{:S(2)}, u32[]{:S(2)}) collective-permute-start(bf16[8,2]{0,1:T(2,128)(2,1)S(1)} %collective-permute-done.12), channel_id=1, source_target_pairs={{0,15},{1,0},{2,1},{3,2},{4,3},{5,4},{6,5},{7,6},{8,7},{9,8},{10,9... | collective-permute-start | bytes 104 | tf_op jit(solution)/shard_map/ppermute | solution.py:24
  214.7 5.7 %collective-permute-start.5 = (bf16[8,2]{0,1:T(2,128)(2,1)S(1)}, bf16[8,2]{0,1:T(2,128)(2,1)S(1)}, u32[]{:S(2)}, u32[]{:S(2)}) collective-permute-start(bf16[8,2]{0,1:T(2,128)(2,1)S(1)} %collective-permute-done.4), channel_id=1, source_target_pairs={{0,1},{1,2},{2,3},{3,4},{4,5},{5,6},{6,7},{7,8},{8,9},{9,10},{10,1... | collective-permute-start | bytes 104 | tf_op jit(solution)/shard_map/ppermute | solution.py:22
  216.0 10.0 %collective-permute-start.14 = (bf16[8,2]{0,1:T(2,128)(2,1)S(1)}, bf16[8,2]{0,1:T(2,128)(2,1)S(1)}, u32[]{:S(2)}, u32[]{:S(2)}) collective-permute-start(bf16[8,2]{0,1:T(2,128)(2,1)S(1)} %collective-permute-done.13), channel_id=1, source_target_pairs={{0,15},{1,0},{2,1},{3,2},{4,3},{5,4},{6,5},{7,6},{8,7},{9,8},{10,9... | collective-permute-start | bytes 104 | tf_op jit(solution)/shard_map/ppermute | solution.py:24
  220.3 5.7 %collective-permute-start.6 = (bf16[8,2]{0,1:T(2,128)(2,1)S(1)}, bf16[8,2]{0,1:T(2,128)(2,1)S(1)}, u32[]{:S(2)}, u32[]{:S(2)}) collective-permute-start(bf16[8,2]{0,1:T(2,128)(2,1)S(1)} %collective-permute-done.5), channel_id=1, source_target_pairs={{0,1},{1,2},{2,3},{3,4},{4,5},{5,6},{6,7},{7,8},{8,9},{9,10},{10,1... | collective-permute-start | bytes 104 | tf_op jit(solution)/shard_map/ppermute | solution.py:22
  226.0 5.7 %collective-permute-start.7 = (bf16[8,2]{0,1:T(2,128)(2,1)S(1)}, bf16[8,2]{0,1:T(2,128)(2,1)S(1)}, u32[]{:S(2)}, u32[]{:S(2)}) collective-permute-start(bf16[8,2]{0,1:T(2,128)(2,1)S(1)} %collective-permute-done.6), channel_id=1, source_target_pairs={{0,1},{1,2},{2,3},{3,4},{4,5},{5,6},{6,7},{7,8},{8,9},{9,10},{10,1... | collective-permute-start | bytes 104 | tf_op jit(solution)/shard_map/ppermute | solution.py:22
  236.6 1.7 copy-start
